TPU v7x, 32 devices: a whole 2x2x4 slice. The times are simulated.
32 devices in a mesh: groups: 2 (over x), tensor: 16 (over z, y, core).
Axes of the slice: x: 2, y: 2, z: 4, core: 2. Of those that a mesh axis runs over, the one named last changes fastest.
Arguments:
- tokens: bfloat16 [64, 8192], P(('groups', 'tensor')), parts along dimension 0, may hold values from -6 to 6
- gate_weight: bfloat16 [8192, 28672], P(None, 'tensor'), may hold values from -0.0625 to 0.0625
- up_weight: bfloat16 [8192, 28672], P(None, 'tensor'), may hold values from -0.0625 to 0.0625
- down_weight: bfloat16 [28672, 8192], P('tensor'), may hold values from -0.03125 to 0.03125
Outputs:
- mixed: bfloat16 [64, 8192], P(('groups', 'tensor')), parts along dimension 0
There are 2 independent parts, one for each index of `groups`. A program takes and returns all parts, laid end to end along the dimension named above; an argument that names none is the same for every part. Nothing has to cross between parts.
All inputs are finite; a program needn't handle non-finite values.
Results may differ from a plain program's by a relative error of at most 0.015.
Values may be sent and summed in bfloat16 or wider, within the bound.
A program may use at most 128 MiB of HBM per device.

v0:
```python
import functools

import jax
import jax.numpy as jnp
import numpy as np
from jax import lax
from jax.experimental import pallas as pl
from jax.experimental.pallas import tpu as pltpu
from jax.sharding import PartitionSpec as P

BLOCK = 32
COLS = 256
PAIRS = 4
SPLIT = 4
DOWNS = 6
CHUNKS = 4
GROUP = 3
LAG = 2
MESH = pl.DeviceIdType.MESH


def swapped(value, axis, stride):
    mask = 2**stride
    pairs = [(source, source ^ mask) for source in range(lax.axis_size(axis))]
    return lax.ppermute(value, axis, pairs)


def walsh(order):
    index = np.arange(order)
    common = index[:, None] & index[None, :]
    parity = common * 0
    for shift in range(max(order.bit_length(), 1)):
        parity = parity ^ common >> shift & 1
    return (1 - 2 * parity).astype(np.float32)


def plain(tokens, gate_weight, up_weight, down_weight):
    devices = lax.axis_size("tensor")
    width = gate_weight.shape[1]
    scale = 1.0 / np.sqrt(devices * BLOCK)
    inner = jnp.asarray(walsh(BLOCK), jnp.float32)
    piece = lax.all_gather(tokens, "tensor", axis=0, tiled=True)
    gate = jnp.dot(piece, gate_weight, preferred_element_type=jnp.float32)
    up = jnp.dot(piece, up_weight, preferred_element_type=jnp.float32)
    hidden = jax.nn.silu(gate) * up
    total = hidden.shape[0]
    local = jnp.einsum(
        "tbr,rs->tbs",
        hidden.reshape(total, width // BLOCK, BLOCK),
        inner,
        precision=lax.Precision.HIGHEST,
    ).reshape(total, width)
    index = lax.axis_index("tensor")
    for level in range(devices.bit_length() - 1):
        partner = swapped(local.astype(jnp.bfloat16), "tensor", level).astype(local.dtype)
        upper = index // (1 << level) % 2
        local = jnp.where(upper == 1, partner - local, local + partner)
    rotated = (local * scale).astype(jnp.bfloat16)
    terms = jnp.dot(rotated, down_weight, preferred_element_type=jnp.float32)
    mixed = lax.psum_scatter(terms, "tensor", scatter_dimension=0, tiled=True)
    return mixed.astype(jnp.bfloat16)


def parity(value, bits):
    total = value & 1
    for shift in range(1, bits):
        total = total ^ ((value >> shift) & 1)
    return total


def kernel(
    n,
    tokens,
    gate,
    up,
    down,
    out,
    gathered,
    lhs,
    acc,
    weights,
    downs,
    signs,
    rows,
    first_out,
    first_in,
    second_out,
    second_in,
    half_out,
    half_in,
    quarter_out,
    quarter_in,
    piece_out,
    piece_in,
    weight_sem,
    down_sem,
    gather_send,
    gather_recv,
    turn_send,
    turn_recv,
    sum_send,
    sum_recv,
):
    f32, bf16 = jnp.float32, jnp.bfloat16
    me = lax.axis_index("tensor")
    own, depth = tokens.shape
    total = n * own
    width = gate.shape[1]
    blocks = width // COLS
    outs = down.shape[1]
    bits = n.bit_length() - 1
    ring = n // 4
    scale = float(1.0 / np.sqrt(n * BLOCK))
    offset = [(i % ring) * 4 + (i // ring % 2) * 2 + i // (2 * ring) for i in range(n)]
    part = depth // SPLIT

    def weight_copy(which, b, piece):
        slot = lax.rem(b, PAIRS)
        source = (gate, up)[which]
        return pltpu.make_async_copy(
            source.at[pl.ds(piece * part, part), pl.ds(pl.multiple_of(b * COLS, COLS), COLS)],
            weights.at[slot, pl.ds(piece * part, part), pl.ds(which * COLS, COLS)],
            weight_sem.at[slot, which, piece],
        )

    def down_copy(b):
        slot = lax.rem(b, DOWNS)
        return pltpu.make_async_copy(
            down.at[pl.ds(pl.multiple_of(b * COLS, COLS), COLS)], downs.at[slot], down_sem.at[slot]
        )

    def start_weights(b):
        for piece in range(SPLIT):
            for which in range(2):
                weight_copy(which, b, piece).start()

    for b in range(min(PAIRS, blocks)):
        start_weights(jnp.int32(b))
    for b in range(min(DOWNS, blocks)):
        down_copy(jnp.int32(b)).start()

    barrier = pltpu.get_barrier_semaphore()
    for i in range(1, n):
        pl.semaphore_signal(barrier, inc=1, device_id={"tensor": me ^ offset[i]}, device_id_type=MESH)
    pl.semaphore_wait(barrier, n - 1)

    def pass_on(source, slot, mask):
        return pltpu.make_async_remote_copy(
            src_ref=source,
            dst_ref=gathered.at[slot],
            send_sem=gather_send.at[slot],
            recv_sem=gather_recv.at[slot],
            device_id={"tensor": me ^ mask},
            device_id_type=MESH,
        )

    sends = []

    def send(source, slot, mask):
        copy = pass_on(source, slot, mask)
        copy.start()
        sends.append(copy)

    for i in range(1, ring):
        send(tokens, i, offset[i])
    send(tokens, ring, 2)
    send(tokens, 2 * ring, 1)

    one = lax.broadcasted_iota(jnp.int32, (COLS, COLS), 0)
    two = lax.broadcasted_iota(jnp.int32, (COLS, COLS), 1)
    sign = (1 - 2 * parity(one & two & (BLOCK - 1), BLOCK.bit_length() - 1)).astype(f32)
    signs[...] = jnp.where((one // BLOCK) == (two // BLOCK), sign, 0.0).astype(bf16)

    order = [ring]
    for i in range(1, ring):
        order.append(i)
        if i > 1:
            order.append(ring + i - 1)
    if ring > 1:
        order.append(2 * ring - 1)
    for i in order:
        pass_on(gathered.at[i], i, 1).wait_recv()
        if i < ring:
            send(gathered.at[i], ring + i, 2)
        send(gathered.at[i], 2 * ring + i, 1)
    for i in range(2 * ring, n):
        pass_on(gathered.at[i], i, 1).wait_recv()

    @pl.loop(0, depth // 1024)
    def _(c):
        columns = pl.ds(pl.multiple_of(c * 1024, 1024), 1024)
        for i in range(n):
            value = tokens[:, columns] if i == 0 else gathered[i, :, columns]
            acc[i * own : (i + 1) * own, columns] = value.astype(f32)
        lhs[:, columns] = acc[:, columns].astype(bf16)

    groups = [(lo, min(lo + GROUP, blocks)) for lo in range(0, blocks, GROUP)]

    def exchange(source, target, which, g):
        lo, hi = groups[g]
        columns = pl.ds(lo * COLS, (hi - lo) * COLS)
        return [
            pltpu.make_async_remote_copy(
                src_ref=source.at[i, :, columns],
                dst_ref=target.at[i, :, columns],
                send_sem=turn_send.at[which, g],
                recv_sem=turn_recv.at[which, g],
                device_id={"tensor": me ^ offset[i]},
                device_id_type=MESH,
            )
            for i in range(1, n)
        ]

    def all_of(source, target, which, g):
        lo, hi = groups[g]
        part_of = (pl.ds(1, n - 1), slice(None), pl.ds(lo * COLS, (hi - lo) * COLS))
        return pltpu.make_async_remote_copy(
            src_ref=source.at[part_of],
            dst_ref=target.at[part_of],
            send_sem=turn_send.at[which, g],
            recv_sem=turn_recv.at[which, g],
            device_id={"tensor": me ^ 1},
            device_id_type=MESH,
        )

    flips = [(1 - 2 * parity(me & offset[i], bits)).astype(f32) for i in range(n)]
    whole = (1 - 2 * parity(me, bits)).astype(f32) * scale

    def across(g):
        all_of(first_out, first_in, 0, g).wait_recv()
        for b in range(*groups[g]):
            columns = pl.ds(b * COLS, COLS)
            values = [first_in[i, :, columns].astype(f32) * flips[i] for i in range(n)]
            step = 1
            while step < n:
                for i in range(n):
                    if not i & step:
                        low, high = values[i], values[i + step]
                        values[i], values[i + step] = low + high, low - high
                step *= 2
            for i in range(n):
                target = second_in if i == 0 else second_out
                target[i, :, columns] = (values[i] * (flips[i] * whole)).astype(bf16)
        for copy in exchange(second_out, second_in, 1, g):
            copy.start()

    def block(b):
        slot = lax.rem(b, PAIRS)
        sums = jnp.zeros((total, 2 * COLS), f32)
        for piece in range(SPLIT):
            rows_of = pl.ds(piece * part, part)
            for which in range(2):
                weight_copy(which, b, piece).wait()
            sums += jnp.dot(lhs[:, rows_of], weights[slot, rows_of, :], preferred_element_type=f32)

        @pl.when(b + PAIRS < blocks)
        def _():
            start_weights(b + PAIRS)

        left, right = sums[:, :COLS], sums[:, COLS:]
        hidden = left / (1.0 + jnp.exp(-left)) * right
        high = hidden.astype(bf16)
        low = (hidden - high.astype(f32)).astype(bf16)
        rows[...] = jnp.dot(high, signs[...], preferred_element_type=f32) + jnp.dot(
            low, signs[...], preferred_element_type=f32
        )
        for i in range(n):
            target = first_in if i == 0 else first_out
            target[i, :, pl.ds(pl.multiple_of(b * COLS, COLS), COLS)] = rows[
                i * own : (i + 1) * own, :
            ].astype(bf16)

    begun = 0
    waiting = []
    for b in range(blocks):
        ends = [g for g, (_, hi) in enumerate(groups) if hi == b + 1]
        due = [g for g in waiting if groups[g][1] + LAG <= b + 1]
        if ends or due or b == blocks - 1:
            pl.loop(begun, b + 1)(block)
            begun = b + 1
        for g in ends:
            for copy in exchange(first_out, first_in, 0, g):
                copy.start()
            waiting.append(g)
        for g in due:
            across(g)
            waiting.remove(g)

    def rotated(b):
        g = b // GROUP
        if b == groups[g][0]:
            all_of(second_out, second_in, 1, g).wait_recv()
        columns = pl.ds(b * COLS, COLS)
        for i in range(n):
            rows[i * own : (i + 1) * own, :] = second_in[i, :, columns].astype(f32)
        down_copy(jnp.int32(b)).wait()
        return rows[...].astype(bf16)

    last_group = groups[-1][0]
    while len(waiting) > 1:
        across(waiting.pop(0))
    early = max(last_group - 1, blocks - DOWNS)
    for b in range(early):
        if waiting and b == min(2, early - 1):
            across(waiting.pop(0))
        value = rotated(b)

        @pl.loop(0, outs // 1024)
        def _(c):
            columns = pl.ds(pl.multiple_of(c * 1024, 1024), 1024)
            term = jnp.dot(value, downs[b % DOWNS, :, columns], preferred_element_type=f32)
            if b:
                term = acc[:, columns] + term
            acc[:, columns] = term

        if b + DOWNS < blocks:
            down_copy(jnp.int32(b + DOWNS)).start()
    while waiting:
        across(waiting.pop(0))

    size = outs // CHUNKS
    half, quarter = total // 2, total // 4

    def sum_copy(level, c, source, target, mask, send_sem, recv_sem):
        return pltpu.make_async_remote_copy(
            src_ref=source,
            dst_ref=target,
            send_sem=send_sem,
            recv_sem=recv_sem,
            device_id={"tensor": me ^ mask},
            device_id_type=MESH,
        )

    def half_copy(c):
        return sum_copy(0, c, half_out.at[c], half_in.at[c], 1, sum_send.at[0, c], sum_recv.at[0, c])

    def quarter_copy(c):
        return sum_copy(
            1, c, quarter_out.at[c], quarter_in.at[c], 2, sum_send.at[1, c], sum_recv.at[1, c]
        )

    def piece_copy(c, i):
        return sum_copy(
            2,
            c,
            piece_out.at[c, i - 1],
            piece_in.at[c, i - 1],
            offset[i],
            sum_send.at[1 + i, c],
            sum_recv.at[1 + i, c],
        )

    last = [(b, rotated(b)) for b in range(early, blocks)]
    for c in range(CHUNKS):
        columns = pl.ds(c * size, size)
        term = acc[:, columns]
        for b, value in last:
            term = term + jnp.dot(value, downs[b % DOWNS, :, columns], preferred_element_type=f32)
        half_out[c] = term[half:].astype(bf16)
        acc[:half, columns] = term[:half]
        half_copy(c).start()
    for c in range(CHUNKS):
        columns = pl.ds(c * size, size)
        half_copy(c).wait_recv()
        term = acc[:half, columns] + half_in[c].astype(f32)
        quarter_out[c] = term[quarter:].astype(bf16)
        acc[:quarter, columns] = term[:quarter]
        quarter_copy(c).start()
    for c in range(CHUNKS):
        columns = pl.ds(c * size, size)
        quarter_copy(c).wait_recv()
        acc[:quarter, columns] = acc[:quarter, columns] + quarter_in[c].astype(f32)
        for i in range(1, ring):
            piece_out[c, i - 1] = acc[i * own : (i + 1) * own, columns].astype(bf16)
            piece_copy(c, i).start()
    for c in range(CHUNKS):
        columns = pl.ds(c * size, size)
        term = acc[:own, columns]
        for i in range(1, ring):
            piece_copy(c, i).wait_recv()
            term = term + piece_in[c, i - 1].astype(f32)
        out[:, columns] = term.astype(bf16)

    for copy in sends:
        copy.wait_send()
    for g in range(len(groups)):
        all_of(first_out, first_in, 0, g).wait_send()
        all_of(second_out, second_in, 1, g).wait_send()
    for c in range(CHUNKS):
        half_copy(c).wait_send()
        quarter_copy(c).wait_send()
        for i in range(1, ring):
            piece_copy(c, i).wait_send()


def fused(n, tokens, gate_weight, up_weight, down_weight):
    own, depth = tokens.shape
    total = n * own
    width = gate_weight.shape[1]
    blocks = width // COLS
    outs = down_weight.shape[1]
    ring = n // 4
    size = outs // CHUNKS
    bf16, f32 = jnp.bfloat16, jnp.float32
    turn = pltpu.VMEM((n, own, width), bf16)
    vmem = pl.BlockSpec(memory_space=pltpu.VMEM)
    anywhere = pl.BlockSpec(memory_space=pl.ANY)
    return pl.pallas_call(
        functools.partial(kernel, n),
        out_shape=jax.ShapeDtypeStruct((own, outs), bf16),
        in_specs=[vmem, anywhere, anywhere, anywhere],
        out_specs=vmem,
        scratch_shapes=[
            pltpu.VMEM((n, own, depth), bf16),
            pltpu.VMEM((total, depth), bf16),
            pltpu.VMEM((total, max(outs, depth)), f32),
            pltpu.VMEM((PAIRS, depth, 2 * COLS), bf16),
            pltpu.VMEM((DOWNS, COLS, outs), bf16),
            pltpu.VMEM((COLS, COLS), bf16),
            pltpu.VMEM((total, COLS), f32),
            turn,
            turn,
            turn,
            turn,
            pltpu.VMEM((CHUNKS, total // 2, size), bf16),
            pltpu.VMEM((CHUNKS, total // 2, size), bf16),
            pltpu.VMEM((CHUNKS, total // 4, size), bf16),
            pltpu.VMEM((CHUNKS, total // 4, size), bf16),
            pltpu.VMEM((CHUNKS, ring - 1, own, size), bf16),
            pltpu.VMEM((CHUNKS, ring - 1, own, size), bf16),
            pltpu.SemaphoreType.DMA((PAIRS, 2, SPLIT)),
            pltpu.SemaphoreType.DMA((DOWNS,)),
            pltpu.SemaphoreType.DMA((n,)),
            pltpu.SemaphoreType.DMA((n,)),
            pltpu.SemaphoreType.DMA((2, pl.cdiv(blocks, GROUP))),
            pltpu.SemaphoreType.DMA((2, pl.cdiv(blocks, GROUP))),
            pltpu.SemaphoreType.DMA((1 + ring, CHUNKS)),
            pltpu.SemaphoreType.DMA((1 + ring, CHUNKS)),
        ],
        compiler_params=pltpu.CompilerParams(
            collective_id=0, has_side_effects=True, vmem_limit_bytes=67_000_000
        ),
    )(tokens, gate_weight, up_weight, down_weight)


def per_device(tokens, gate_weight, up_weight, down_weight):
    n = lax.axis_size("tensor")
    own, depth = tokens.shape
    width, outs = gate_weight.shape[1], down_weight.shape[1]
    held = 2 * COLS * (2 * PAIRS * depth + DOWNS * outs)
    fits = (
        8 <= n
        and n & (n - 1) == 0
        and width % COLS == 0
        and width // COLS > max(PAIRS, LAG, GROUP, DOWNS)
        and n * own % 32 == 0
        and n * own <= 64
        and depth % (1024 * SPLIT) == 0
        and outs % (1024 * CHUNKS) == 0
        and held <= 60 << 20
    )
    if fits:
        return fused(n, tokens, gate_weight, up_weight, down_weight)
    return plain(tokens, gate_weight, up_weight, down_weight)


def solution(mesh):
    return jax.shard_map(
        per_device,
        mesh=mesh,
        in_specs=(
            P(("groups", "tensor"), None),
            P(None, "tensor"),
            P(None, "tensor"),
            P("tensor", None),
        ),
        out_specs=P(("groups", "tensor"), None),
        check_vma=False,
    )
```

profile of v0, /device:TPU:0, one launch (start us, length us, event | category | flops | bytes accessed | tf_op | source)
XLA Modules:
  0.0 54.0 jit_solution(8072982389890287334)
XLA Ops:
  0.0 52.6 %shard_map.46 = bf16[2,8192]{1,0:T(2,128)(2,1)} custom-call(bf16[2,8192]{1,0:T(2,128)(2,1)} %tokens.1, bf16[8192,1792]{1,0:T(8,128)(2,1)} %gate.1, bf16[8192,1792]{1,0:T(8,128)(2,1)} %up.1, bf16[1792,8192]{1,0:T(8,128)(2,1)} %down.1), custom_call_target="tpu_custom_call" | custom-call | tf_op jit(solution)/shard_map/pallas_call | solution.py:408
  52.6 1.4 %copy.6 = bf16[2,8192]{1,0:T(2,128)(2,1)} copy(bf16[2,8192]{1,0:T(2,128)(2,1)} %shard_map.46) | data formatting | bytes 65536
where the time goes:
time: 54.3 us; the launch traced here: 54 us
  Pallas kernels  52.6 us (97%)
  local copies, waits for them, and re-layouts  1.4 us (3%)
    pallas_call x1, Pallas kernels, fused(): pl.pallas_call(functools.partial(kernel, n), out_shape=jax.ShapeDtypeStru...  52.6 us
    unnamed x1, local copies, waits for them, and re-layouts  1.4 us

commit v1 on v0

v1 whole, which is shorter than its diff:
```python
import functools

import jax
import jax.numpy as jnp
import numpy as np
from jax import lax
from jax.experimental import pallas as pl
from jax.experimental.pallas import tpu as pltpu
from jax.sharding import PartitionSpec as P

BLOCK = 32
COLS = 128
SPLIT = 4
CHUNKS = 4
GROUP = 2
PLANE = 4
MESH = pl.DeviceIdType.MESH


def swapped(value, axis, stride):
    mask = 2**stride
    pairs = [(source, source ^ mask) for source in range(lax.axis_size(axis))]
    return lax.ppermute(value, axis, pairs)


def walsh(order):
    index = np.arange(order)
    common = index[:, None] & index[None, :]
    parity = common * 0
    for shift in range(max(order.bit_length(), 1)):
        parity = parity ^ common >> shift & 1
    return (1 - 2 * parity).astype(np.float32)


def plain(tokens, gate_weight, up_weight, down_weight):
    devices = lax.axis_size("tensor")
    width = gate_weight.shape[1]
    scale = 1.0 / np.sqrt(devices * BLOCK)
    inner = jnp.asarray(walsh(BLOCK), jnp.float32)
    piece = lax.all_gather(tokens, "tensor", axis=0, tiled=True)
    gate = jnp.dot(piece, gate_weight, preferred_element_type=jnp.float32)
    up = jnp.dot(piece, up_weight, preferred_element_type=jnp.float32)
    hidden = jax.nn.silu(gate) * up
    total = hidden.shape[0]
    local = jnp.einsum(
        "tbr,rs->tbs",
        hidden.reshape(total, width // BLOCK, BLOCK),
        inner,
        precision=lax.Precision.HIGHEST,
    ).reshape(total, width)
    index = lax.axis_index("tensor")
    for level in range(devices.bit_length() - 1):
        partner = swapped(local.astype(jnp.bfloat16), "tensor", level).astype(local.dtype)
        upper = index // (1 << level) % 2
        local = jnp.where(upper == 1, partner - local, local + partner)
    rotated = (local * scale).astype(jnp.bfloat16)
    terms = jnp.dot(rotated, down_weight, preferred_element_type=jnp.float32)
    mixed = lax.psum_scatter(terms, "tensor", scatter_dimension=0, tiled=True)
    return mixed.astype(jnp.bfloat16)


def parity(value, bits):
    total = value & 1
    for shift in range(1, bits):
        total = total ^ ((value >> shift) & 1)
    return total


def kernel(
    n,
    tokens,
    gate,
    up,
    down,
    out,
    gathered,
    lhs,
    acc,
    weights,
    downs,
    signs,
    hidden,
    first_out,
    first_in,
    middle,
    second_out,
    second_in,
    rotated,
    half_out,
    half_in,
    piece_out,
    piece_in,
    weight_sem,
    down_sem,
    gather_send,
    gather_recv,
    first_send,
    first_recv,
    second_send,
    second_recv,
    half_send,
    half_recv,
    piece_send,
    piece_recv,
):
    f32, bf16 = jnp.float32, jnp.bfloat16
    me = lax.axis_index("tensor")
    mine = lax.axis_index("groups")
    own, depth = tokens.shape
    total = n * own
    part = gate.shape[1] // 2
    blocks = part // COLS
    outs = down.shape[1]
    bits = n.bit_length() - 1
    ring = n // PLANE
    scale = float(1.0 / np.sqrt(n * BLOCK))
    deep = depth // SPLIT

    def device(j, mask):
        return {"groups": mine ^ j, "tensor": me ^ mask}

    def slot(j, mask):
        q = me ^ mask
        return (mine ^ j) * n + (q & 1) * (n // 2) + (q >> 1)

    def remote(source, target, send_sem, recv_sem, j, mask):
        return pltpu.make_async_remote_copy(
            src_ref=source,
            dst_ref=target,
            send_sem=send_sem,
            recv_sem=recv_sem,
            device_id=device(j, mask),
            device_id_type=MESH,
        )

    plane = [(j, m) for j in range(2) for m in range(PLANE) if j or m]
    line = [(0, PLANE * k) for k in range(1, ring)]

    barrier = pltpu.get_barrier_semaphore()
    for j, mask in plane + line:
        pl.semaphore_signal(barrier, inc=1, device_id=device(j, mask), device_id_type=MESH)

    def weight_copy(which, b):
        source = (gate, up)[which]
        start = pl.multiple_of(mine * part + b * COLS, COLS)
        return pltpu.make_async_copy(
            source.at[:, pl.ds(start, COLS)],
            weights.at[b, :, pl.ds(which * COLS, COLS)],
            weight_sem.at[b, which],
        )

    def down_copy(b, j):
        start = pl.multiple_of((mine ^ j) * part + b * COLS, COLS)
        return pltpu.make_async_copy(
            down.at[pl.ds(start, COLS)], downs.at[pl.ds((2 * b + j) * COLS, COLS)], down_sem.at[b, j]
        )

    for b in range(blocks):
        for which in range(2):
            weight_copy(which, b).start()

    pl.semaphore_wait(barrier, len(plane) + len(line))

    sends = []

    def send(source, place, origin, j, mask):
        oj, om = origin[0] ^ j, origin[1] ^ mask
        copy = remote(
            source,
            gathered.at[place],
            gather_send.at[len(sends)],
            gather_recv.at[oj * n + om],
            j,
            mask,
        )
        copy.start()
        sends.append(copy)

    def arrived(j, mask):
        place = slot(j, mask)
        remote(
            gathered.at[place], gathered.at[place], gather_send.at[0], gather_recv.at[j * n + mask], 0, 1
        ).wait_recv()
        return place

    here = slot(0, 0)
    near = [(1, 0), (0, 2), (1, 2)]
    for j, mask in line[::-1] + near + [(0, 1)]:
        send(tokens, here, (0, 0), j, mask)
    gathered[here] = tokens[...]

    one = lax.broadcasted_iota(jnp.int32, (COLS, COLS), 0)
    two = lax.broadcasted_iota(jnp.int32, (COLS, COLS), 1)
    sign = (1 - 2 * parity(one & two & (BLOCK - 1), BLOCK.bit_length() - 1)).astype(f32)
    signs[...] = jnp.where((one // BLOCK) == (two // BLOCK), sign, 0.0).astype(bf16)

    def to_core(j, mask):
        place = arrived(j, mask)
        send(gathered.at[place], place, (j, mask), 0, 1)

    def spread(k):
        place = arrived(0, PLANE * k)
        for j, mask in near + [(0, 1)]:
            send(gathered.at[place], place, (0, PLANE * k), j, mask)

    for k in range(1, ring):
        spread(k)
        if k == 1:
            for j, mask in near:
                to_core(j, mask)
    for b in range(blocks):
        for j in range(2):
            down_copy(b, j).start()
    for k in range(1, ring):
        for j, mask in near:
            to_core(j, PLANE * k + mask)
    for k in range(ring):
        for j, mask in [(0, 1), (1, 1), (0, 3), (1, 3)]:
            arrived(j, PLANE * k + mask)

    @pl.loop(0, depth // 1024)
    def _(c):
        columns = pl.ds(pl.multiple_of(c * 1024, 1024), 1024)
        lhs[:, columns] = gathered[:, :, columns].reshape(2 * total, 1024)

    groups = [(lo, min(lo + GROUP, blocks)) for lo in range(0, blocks, GROUP)]

    def first_copy(g, j, m):
        lo, hi = groups[g]
        columns = pl.ds(lo * COLS, (hi - lo) * COLS)
        place = j * PLANE + m
        return remote(
            first_out.at[mine ^ j, :, columns],
            first_in.at[place, :, columns],
            first_send.at[g, place],
            first_recv.at[g, place],
            j,
            m,
        )

    def second_copy(g, k):
        lo, hi = groups[g]
        columns = pl.ds(2 * lo * COLS, 2 * (hi - lo) * COLS)
        return remote(
            second_out.at[:, columns],
            second_in.at[k, :, columns],
            second_send.at[g, k],
            second_recv.at[g, k],
            0,
            PLANE * k,
        )

    def flip(mask, kept):
        return (1 - 2 * parity(me & (me ^ mask) & kept, bits)).astype(f32)

    plane_flips = [flip(m, PLANE - 1) for m in range(PLANE)]
    line_flips = [flip(PLANE * k, n - PLANE) * scale for k in range(ring)]

    def block(b):
        left = jnp.zeros((2 * total, COLS), f32)
        right = jnp.zeros((2 * total, COLS), f32)
        for which in range(2):
            weight_copy(which, b).wait()
        for piece in range(SPLIT):
            rows_of = pl.ds(piece * deep, deep)
            left += jnp.dot(lhs[:, rows_of], weights[b, rows_of, :COLS], preferred_element_type=f32)
            right += jnp.dot(lhs[:, rows_of], weights[b, rows_of, COLS:], preferred_element_type=f32)
        value = left / (1.0 + jnp.exp(-left)) * right
        high = value.astype(bf16)
        low = (value - high.astype(f32)).astype(bf16)
        value = jnp.dot(high, signs[...], preferred_element_type=f32) + jnp.dot(
            low, signs[...], preferred_element_type=f32
        )
        columns = pl.ds(b * COLS, COLS)
        for j in range(2):
            hidden[j, :, columns] = value[j * total : (j + 1) * total]
            first_out[j, :, columns] = value[j * total : (j + 1) * total].astype(bf16)

    for g, (lo, hi) in enumerate(groups):
        for b in range(lo, hi):
            block(b)
        for j, m in plane[::-1]:
            first_copy(g, j, m).start()

    for g, (lo, hi) in enumerate(groups):
        for j, m in plane:
            first_copy(g, j, m).wait_recv()
        for b in range(lo, hi):
            columns = pl.ds(b * COLS, COLS)
            for j in range(2):
                value = None
                for m in range(PLANE):
                    if j or m:
                        piece = first_in[j * PLANE + m, :, columns].astype(f32)
                    else:
                        piece = hidden[mine, :, columns]
                    piece = piece * plane_flips[m]
                    value = piece if value is None else value + piece
                target = pl.ds((2 * b + j) * COLS, COLS)
                middle[:, target] = value
                second_out[:, target] = value.astype(bf16)
        for k in range(ring - 1, 0, -1):
            second_copy(g, k).start()

    def rotate(g):
        lo, hi = groups[g]
        for k in range(1, ring):
            second_copy(g, k).wait_recv()
        for b in range(2 * lo, 2 * hi):
            columns = pl.ds(b * COLS, COLS)
            value = middle[:, columns] * line_flips[0]
            for k in range(1, ring):
                value = value + second_in[k, :, columns].astype(f32) * line_flips[k]
            rotated[:, columns] = value.astype(bf16)
        for b in range(lo, hi):
            for j in range(2):
                down_copy(b, j).wait()

    def product(g, columns):
        lo, hi = groups[g]
        rows_of = pl.ds(2 * lo * COLS, 2 * (hi - lo) * COLS)
        return jnp.dot(rotated[:, rows_of], downs[rows_of, columns], preferred_element_type=f32)

    last = len(groups) - 1
    for g in range(last):
        rotate(g)

        @pl.loop(0, outs // 2048)
        def _(c):
            columns = pl.ds(pl.multiple_of(c * 2048, 2048), 2048)
            term = product(g, columns)
            if g:
                term = acc[:, columns] + term
            acc[:, columns] = term

    size = outs // CHUNKS
    half = total // 2
    pieces = n // 2
    place = me >> 1
    kept = pl.ds(pl.multiple_of((me & 1) * half, half), half)
    given = pl.ds(pl.multiple_of((1 - (me & 1)) * half, half), half)

    def half_copy(c):
        columns = pl.ds(c * size, size)
        return remote(
            half_out.at[:, columns], half_in.at[:, columns], half_send.at[c], half_recv.at[c], 0, 1
        )

    def piece_copy(c, k):
        columns = pl.ds(c * size, size)
        return remote(
            piece_out.at[place ^ k, :, columns],
            piece_in.at[k, :, columns],
            piece_send.at[c, k],
            piece_recv.at[c, k],
            0,
            2 * k,
        )

    rotate(last)
    for c in range(CHUNKS):
        columns = pl.ds(c * size, size)
        acc[:, columns] = acc[:, columns] + product(last, columns)
        half_out[:, columns] = acc[given, columns].astype(bf16)
        half_copy(c).start()
    for c in range(CHUNKS):
        columns = pl.ds(c * size, size)
        half_copy(c).wait_recv()
        term = acc[kept, columns] + half_in[:, columns].astype(f32)
        piece_out[:, :, columns] = term.astype(bf16).reshape(pieces, own, size)
        for k in range(pieces - 1, 0, -1):
            piece_copy(c, k).start()
    for c in range(CHUNKS):
        columns = pl.ds(c * size, size)
        term = piece_out[place, :, columns].astype(f32)
        for k in range(1, pieces):
            piece_copy(c, k).wait_recv()
            term = term + piece_in[k, :, columns].astype(f32)
        out[:, columns] = term.astype(bf16)

    for copy in sends:
        copy.wait_send()
    for g in range(len(groups)):
        for j, m in plane:
            first_copy(g, j, m).wait_send()
        for k in range(1, ring):
            second_copy(g, k).wait_send()
    for c in range(CHUNKS):
        half_copy(c).wait_send()
        for k in range(1, pieces):
            piece_copy(c, k).wait_send()


def fused(n, tokens, gate_weight, up_weight, down_weight):
    own, depth = tokens.shape
    total = n * own
    part = gate_weight.shape[1] // 2
    blocks = part // COLS
    outs = down_weight.shape[1]
    ring = n // PLANE
    pieces = n // 2
    groups = pl.cdiv(blocks, GROUP)
    bf16, f32 = jnp.bfloat16, jnp.float32
    vmem = pl.BlockSpec(memory_space=pltpu.VMEM)
    anywhere = pl.BlockSpec(memory_space=pl.ANY)
    dma = pltpu.SemaphoreType.DMA
    sent = (ring - 1) * 5 + 4 + (PLANE - 1) * ring
    return pl.pallas_call(
        functools.partial(kernel, n),
        out_shape=jax.ShapeDtypeStruct((own, outs), bf16),
        in_specs=[vmem, anywhere, anywhere, anywhere],
        out_specs=vmem,
        scratch_shapes=[
            pltpu.VMEM((2 * n, own, depth), bf16),
            pltpu.VMEM((2 * total, depth), bf16),
            pltpu.VMEM((total, outs), f32),
            pltpu.VMEM((blocks, depth, 2 * COLS), bf16),
            pltpu.VMEM((2 * part, outs), bf16),
            pltpu.VMEM((COLS, COLS), bf16),
            pltpu.VMEM((2, total, part), f32),
            pltpu.VMEM((2, total, part), bf16),
            pltpu.VMEM((2 * PLANE, total, part), bf16),
            pltpu.VMEM((total, 2 * part), f32),
            pltpu.VMEM((total, 2 * part), bf16),
            pltpu.VMEM((ring, total, 2 * part), bf16),
            pltpu.VMEM((total, 2 * part), bf16),
            pltpu.VMEM((total // 2, outs), bf16),
            pltpu.VMEM((total // 2, outs), bf16),
            pltpu.VMEM((pieces, own, outs), bf16),
            pltpu.VMEM((pieces, own, outs), bf16),
            dma((blocks, 2)),
            dma((blocks, 2)),
            dma((sent,)),
            dma((2 * n,)),
            dma((groups, 2 * PLANE)),
            dma((groups, 2 * PLANE)),
            dma((groups, ring)),
            dma((groups, ring)),
            dma((CHUNKS,)),
            dma((CHUNKS,)),
            dma((CHUNKS, pieces)),
            dma((CHUNKS, pieces)),
        ],
        compiler_params=pltpu.CompilerParams(
            collective_id=0, has_side_effects=True, vmem_limit_bytes=67_000_000
        ),
    )(tokens, gate_weight, up_weight, down_weight)


def per_device(tokens, gate_weight, up_weight, down_weight):
    n, parts = lax.axis_size("tensor"), lax.axis_size("groups")
    own, depth = tokens.shape
    width, outs = gate_weight.shape[1], down_weight.shape[1]
    total = n * own
    held = 2 * (width * (depth + outs) + 4 * total * (depth + outs) + 20 * total * width)
    fits = (
        parts == 2
        and 8 <= n
        and n & (n - 1) == 0
        and width % (2 * COLS) == 0
        and width // (2 * COLS) > GROUP
        and total % 32 == 0
        and total <= 64
        and depth % (1024 * SPLIT) == 0
        and outs % (2048 * CHUNKS) == 0
        and held <= 68_000_000
    )
    if fits:
        return fused(n, tokens, gate_weight, up_weight, down_weight)
    return plain(tokens, gate_weight, up_weight, down_weight)


def solution(mesh):
    return jax.shard_map(
        per_device,
        mesh=mesh,
        in_specs=(
            P(("groups", "tensor"), None),
            P(None, "tensor"),
            P(None, "tensor"),
            P("tensor", None),
        ),
        out_specs=P(("groups", "tensor"), None),
        check_vma=False,
    )
```

time: 54.3 us -> 49.8 us (0.917)
  Pallas kernels: 52.6 us -> 48.1 us
    pallas_call x1, Pallas kernels: 52.6 us -> 48.1 us  [fused(): pl.pallas_call(functools.partial(kernel, n), out_shape=jax.ShapeDtypeStru...]
where the time goes in v1:
time: 49.8 us; the launch traced here: 49.5 us
  Pallas kernels  48.1 us (97%)
  local copies, waits for them, and re-layouts  1.4 us (3%)
    pallas_call x1, Pallas kernels, fused(): pl.pallas_call(functools.partial(kernel, n), out_shape=jax.ShapeDtypeStru...  48.1 us
    unnamed x1, local copies, waits for them, and re-layouts  1.4 us

profile of v1, /device:TPU:0, one launch (start us, length us, event | category | flops | bytes accessed | tf_op | source)
XLA Modules:
  0.0 49.5 jit_solution(6416199906458128503)
XLA Ops:
  0.0 48.1 %shard_map.46 = bf16[2,8192]{1,0:T(2,128)(2,1)} custom-call(bf16[2,8192]{1,0:T(2,128)(2,1)} %tokens.1, bf16[8192,1792]{1,0:T(8,128)(2,1)} %gate.1, bf16[8192,1792]{1,0:T(8,128)(2,1)} %up.1, bf16[1792,8192]{1,0:T(8,128)(2,1)} %down.1), custom_call_target="tpu_custom_call" | custom-call | tf_op jit(solution)/shard_map/pallas_call | solution.py:408
  48.1 1.4 %copy.6 = bf16[2,8192]{1,0:T(2,128)(2,1)} copy(bf16[2,8192]{1,0:T(2,128)(2,1)} %shard_map.46) | data formatting | bytes 65536

commit v2 on v1

v2 whole, which is shorter than its diff:
```python
import functools

import jax
import jax.numpy as jnp
import numpy as np
from jax import lax
from jax.experimental import pallas as pl
from jax.experimental.pallas import tpu as pltpu
from jax.sharding import PartitionSpec as P

BLOCK = 32
COLS = 128
SPLIT = 4
CHUNKS = 4
GROUP = 2
LAG = 1
QUADS = (0, 3)
PLANE = 4
MESH = pl.DeviceIdType.MESH


def swapped(value, axis, stride):
    mask = 2**stride
    pairs = [(source, source ^ mask) for source in range(lax.axis_size(axis))]
    return lax.ppermute(value, axis, pairs)


def walsh(order):
    index = np.arange(order)
    common = index[:, None] & index[None, :]
    parity = common * 0
    for shift in range(max(order.bit_length(), 1)):
        parity = parity ^ common >> shift & 1
    return (1 - 2 * parity).astype(np.float32)


def plain(tokens, gate_weight, up_weight, down_weight):
    devices = lax.axis_size("tensor")
    width = gate_weight.shape[1]
    scale = 1.0 / np.sqrt(devices * BLOCK)
    inner = jnp.asarray(walsh(BLOCK), jnp.float32)
    piece = lax.all_gather(tokens, "tensor", axis=0, tiled=True)
    gate = jnp.dot(piece, gate_weight, preferred_element_type=jnp.float32)
    up = jnp.dot(piece, up_weight, preferred_element_type=jnp.float32)
    hidden = jax.nn.silu(gate) * up
    total = hidden.shape[0]
    local = jnp.einsum(
        "tbr,rs->tbs",
        hidden.reshape(total, width // BLOCK, BLOCK),
        inner,
        precision=lax.Precision.HIGHEST,
    ).reshape(total, width)
    index = lax.axis_index("tensor")
    for level in range(devices.bit_length() - 1):
        partner = swapped(local.astype(jnp.bfloat16), "tensor", level).astype(local.dtype)
        upper = index // (1 << level) % 2
        local = jnp.where(upper == 1, partner - local, local + partner)
    rotated = (local * scale).astype(jnp.bfloat16)
    terms = jnp.dot(rotated, down_weight, preferred_element_type=jnp.float32)
    mixed = lax.psum_scatter(terms, "tensor", scatter_dimension=0, tiled=True)
    return mixed.astype(jnp.bfloat16)


def parity(value, bits):
    total = value & 1
    for shift in range(1, bits):
        total = total ^ ((value >> shift) & 1)
    return total


def kernel(
    n,
    tokens,
    gate,
    up,
    down,
    out,
    gathered,
    lhs,
    acc,
    weights,
    downs,
    signs,
    hidden,
    core_out,
    core_in,
    first_out,
    first_in,
    middle,
    second_out,
    second_in,
    rotated,
    half_out,
    half_in,
    piece_out,
    piece_in,
    weight_sem,
    down_sem,
    gather_sem,
    core_sem,
    first_sem,
    second_sem,
    half_sem,
    piece_sem,
    send_sem,
    known,
):
    f32, bf16 = jnp.float32, jnp.bfloat16
    me = lax.axis_index("tensor")
    mine = lax.axis_index("groups")
    own, depth = tokens.shape
    total = n * own
    part = gate.shape[1] // 2
    blocks = part // COLS
    outs = down.shape[1]
    bits = n.bit_length() - 1
    ring = n // PLANE
    levels = ring.bit_length() - 1
    scale = float(1.0 / np.sqrt(n * BLOCK))
    deep = depth // SPLIT
    groups = [(lo, min(lo + GROUP, blocks)) for lo in range(0, blocks, GROUP)]
    every = range(len(groups))
    at_gather, at_core, at_first, at_half, at_piece, at_second = range(6)
    quads = [g in QUADS or levels == 1 for g in every]

    def device(j, mask):
        return {"groups": mine ^ j, "tensor": me ^ mask}

    def slot(j, mask):
        q = me ^ mask
        return (mine ^ j) * n + (q & 1) * (n // 2) + (q >> 1)

    def remote(source, target, sent, received, j, mask):
        return pltpu.make_async_remote_copy(
            src_ref=source,
            dst_ref=target,
            send_sem=send_sem.at[sent],
            recv_sem=received,
            device_id=device(j, mask),
            device_id_type=MESH,
        )

    plane = [(j, m) for j in range(2) for m in range(PLANE) if j or m]
    line = [(0, PLANE * k) for k in range(1, ring)]

    barrier = pltpu.get_barrier_semaphore()
    greeted = plane + line[:2]
    for j, mask in greeted:
        pl.semaphore_signal(barrier, inc=1, device_id=device(j, mask), device_id_type=MESH)

    for g, (lo, hi) in enumerate(groups):
        for b in range(lo, hi):
            start = pl.multiple_of(mine * part + b * COLS, COLS)
            for which, source in enumerate((gate, up)):
                pltpu.make_async_copy(
                    source.at[:, pl.ds(start, COLS)],
                    weights.at[b, :, pl.ds(which * COLS, COLS)],
                    weight_sem.at[g],
                ).start()

    def down_rows(g):
        lo, hi = groups[g]
        return pl.ds(2 * lo * COLS, 2 * (hi - lo) * COLS)

    def start_downs():
        for g, (lo, hi) in enumerate(groups):
            for b in range(lo, hi):
                for j in range(2):
                    start = pl.multiple_of((mine ^ j) * part + b * COLS, COLS)
                    pltpu.make_async_copy(
                        down.at[pl.ds(start, COLS)],
                        downs.at[pl.ds((2 * b + j) * COLS, COLS)],
                        down_sem.at[g],
                    ).start()

    pl.semaphore_wait(barrier, len(greeted))
    for j, mask in line[2:]:
        pl.semaphore_signal(known, inc=1, device_id=device(0, PLANE), device_id_type=MESH)

    near = [(1, 0), (0, 2), (1, 2)]
    across = near[:2]
    diagonal = near[2]
    ours = ring
    aside = 2 * ring
    last_sem = 2 * ring + 1
    kinds = {}
    for k in range(ring):
        for j, m in [(0, 0)] + near:
            if (j, m) == (0, 0):
                kind = k
            elif (j, m) != diagonal:
                kind = ours + k
            else:
                kind = aside if k else 0
            kinds[j, PLANE * k + m] = kind
            kinds[j, PLANE * k + m ^ 1] = last_sem
    sends = []

    def send(origin, j, mask):
        place = slot(*origin)
        kind = kinds[origin[0] ^ j, origin[1] ^ mask]
        source = gathered.at[place] if any(origin) else tokens
        remote(source, gathered.at[place], at_gather, gather_sem.at[kind], j, mask).start()
        sends.append(origin)

    def arrived(kind, count):
        some = gathered.at[pl.ds(0, count)]
        remote(some, some, at_gather, gather_sem.at[kind], 0, 1).wait_recv()

    for j, mask in [diagonal] + line[:2][::-1] + across + [(0, 1)]:
        send((0, 0), j, mask)
    gathered[slot(0, 0)] = tokens[...]
    for j, mask in line[2:]:
        pl.semaphore_wait(known, 1)
        send((0, 0), j, mask)

    one = lax.broadcasted_iota(jnp.int32, (COLS, COLS), 0)
    two = lax.broadcasted_iota(jnp.int32, (COLS, COLS), 1)
    sign = (1 - 2 * parity(one & two & (BLOCK - 1), BLOCK.bit_length() - 1)).astype(f32)
    signs[...] = jnp.where((one // BLOCK) == (two // BLOCK), sign, 0.0).astype(bf16)

    def spread(k):
        arrived(k, 1)
        for j, mask in across:
            send((0, PLANE * k), j, mask)
        if k == ring - 1:
            for j, mask in across:
                send((0, PLANE * k), j, mask ^ 1)
        send((0, PLANE * k), 0, 1)

    def from_across(k):
        arrived(ours + k, 2)
        if k == 0 or k < ring - 1:
            for j, mask in across:
                send((j, PLANE * k + mask), 0, 1)

    spread(1)
    arrived(0, 1)
    for j, mask in line[::-1] + [(0, 1)]:
        send(diagonal, j, mask)
    from_across(0)
    for k in range(2, ring):
        spread(k)
    start_downs()
    for k in range(1, ring):
        from_across(k)
    arrived(aside, ring - 1)
    for k in range(1, ring):
        send((diagonal[0], PLANE * k + diagonal[1]), 0, 1)
    arrived(last_sem, n)

    for g, (lo, hi) in enumerate(groups):
        some = weights.at[lo:hi]
        pltpu.make_async_copy(some, some, weight_sem.at[g]).wait()

    @pl.loop(0, depth // 1024)
    def _(c):
        columns = pl.ds(pl.multiple_of(c * 1024, 1024), 1024)
        lhs[:, columns] = gathered[:, :, columns].reshape(2 * total, 1024)

    def core_copy(b):
        columns = pl.ds(b * COLS, COLS)
        return remote(
            core_out.at[:, :, columns], core_in.at[:, :, columns], at_core, core_sem.at[b], 0, 1
        )

    def first_columns(g):
        lo, hi = groups[g]
        return pl.ds(lo * COLS, (hi - lo) * COLS)

    def second_copy(g, level):
        columns = down_rows(g)
        return remote(
            second_out.at[level, :, columns],
            second_in.at[level, :, columns],
            at_second + g,
            second_sem.at[g, level],
            0,
            PLANE << level,
        )

    def quad_copy(g, k):
        columns = down_rows(g)
        return remote(
            second_out.at[0, :, columns],
            second_in.at[k - 1, :, columns],
            at_second + g,
            second_sem.at[g, 0],
            0,
            PLANE * k,
        )

    def flip(mask):
        return (1 - 2 * parity(me & mask, bits)).astype(f32)

    core_flip, row_flip = flip(1), flip(2)
    line_flips = [flip(PLANE << level) for level in range(levels)]

    def project(b):
        left = jnp.zeros((2 * total, COLS), f32)
        right = jnp.zeros((2 * total, COLS), f32)
        for piece in range(SPLIT):
            rows_of = pl.ds(piece * deep, deep)
            left += jnp.dot(lhs[:, rows_of], weights[b, rows_of, :COLS], preferred_element_type=f32)
            right += jnp.dot(lhs[:, rows_of], weights[b, rows_of, COLS:], preferred_element_type=f32)
        return left, right

    def block(b, left, right):
        value = left / (1.0 + jnp.exp(-left)) * right
        high = value.astype(bf16)
        low = (value - high.astype(f32)).astype(bf16)
        value = jnp.dot(high, signs[...], preferred_element_type=f32) + jnp.dot(
            low, signs[...], preferred_element_type=f32
        )
        columns = pl.ds(b * COLS, COLS)
        for j in range(2):
            hidden[j, :, columns] = value[j * total : (j + 1) * total]
            core_out[j, :, columns] = value[j * total : (j + 1) * total].astype(bf16)
        core_copy(b).start()

    def join(b):
        core_copy(b).wait_recv()
        columns = pl.ds(b * COLS, COLS)
        for j in range(2):
            value = hidden[j, :, columns] * core_flip + core_in[j, :, columns].astype(f32)
            hidden[j, :, columns] = value
            first_out[j, :, columns] = value.astype(bf16)
        for g, (lo, hi) in enumerate(groups):
            if b == hi - 1:
                for place in (2, 0, 1):
                    j, m = near[place]
                    remote(
                        first_out.at[mine ^ j, :, first_columns(g)],
                        first_in.at[place, :, first_columns(g)],
                        at_first,
                        first_sem.at[g],
                        j,
                        m,
                    ).start()

    def meet(g):
        some = first_in.at[:, :, first_columns(g)]
        remote(some, some, at_first, first_sem.at[g], 0, 1).wait_recv()
        for b in range(*groups[g]):
            columns = pl.ds(b * COLS, COLS)
            pair = [
                hidden[mine, :, columns] * row_flip + first_in[1, :, columns].astype(f32),
                first_in[0, :, columns].astype(f32) * row_flip + first_in[2, :, columns].astype(f32),
            ]
            for j, value in enumerate(pair):
                target = pl.ds((2 * b + j) * COLS, COLS)
                middle[:, target] = value
                second_out[0, :, target] = value.astype(bf16)
        if quads[g]:
            for k in range(ring - 1, 0, -1):
                quad_copy(g, k).start()
        else:
            second_copy(g, 0).start()

    def gain(mask):
        return (1 - 2 * parity(me & (me ^ mask) & (n - PLANE), bits)).astype(f32) * scale

    gains = [gain(PLANE * k) for k in range(ring)]

    def turn_quad(g):
        some = second_in.at[:, :, down_rows(g)]
        remote(some, some, at_second + g, second_sem.at[g, 0], 0, PLANE).wait_recv()
        for b in range(2 * groups[g][0], 2 * groups[g][1]):
            columns = pl.ds(b * COLS, COLS)
            value = middle[:, columns] * gains[0]
            for k in range(1, ring):
                value = value + second_in[k - 1, :, columns].astype(f32) * gains[k]
            rotated[:, columns] = value.astype(bf16)

    def turn(g, level):
        lo, hi = groups[g]
        second_copy(g, level).wait_recv()
        for b in range(2 * lo, 2 * hi):
            columns = pl.ds(b * COLS, COLS)
            value = middle[:, columns] * line_flips[level]
            value = value + second_in[level, :, columns].astype(f32)
            if level == levels - 1:
                rotated[:, columns] = (value * scale).astype(bf16)
            else:
                middle[:, columns] = value
                second_out[level + 1, :, columns] = value.astype(bf16)
        if level < levels - 1:
            second_copy(g, level + 1).start()

    ready = project(0)
    for b in range(blocks):
        later = project(b + 1) if b + 1 < blocks else None
        block(b, *ready)
        ready = later
        if b >= LAG:
            join(b - LAG)
    for b in range(max(blocks - LAG, 0), blocks):
        join(b)

    steps = [(0.6 * hi + 3.0 * stage, stage, g) for stage in range(levels) for g, (_, hi) in enumerate(groups)]
    for _, stage, g in sorted(steps):
        if stage:
            if not quads[g]:
                turn(g, stage - 1)
        else:
            meet(g)

    def rotate(g):
        if quads[g]:
            turn_quad(g)
        else:
            turn(g, levels - 1)
        some = downs.at[down_rows(g)]
        pltpu.make_async_copy(some, some, down_sem.at[g]).wait()

    def product(g, columns):
        return jnp.dot(rotated[:, down_rows(g)], downs[down_rows(g), columns], preferred_element_type=f32)

    final = len(groups) - 1
    for g in range(final):
        rotate(g)
        for c in range(outs // 1024):
            columns = pl.ds(c * 1024, 1024)
            term = product(g, columns)
            if g:
                term = acc[:, columns] + term
            acc[:, columns] = term

    size = outs // CHUNKS
    half = total // 2
    pieces = n // 2
    place = me >> 1
    kept = pl.ds(pl.multiple_of((me & 1) * half, half), half)
    given = pl.ds(pl.multiple_of((1 - (me & 1)) * half, half), half)

    def half_copy(c):
        columns = pl.ds(c * size, size)
        return remote(half_out.at[:, columns], half_in.at[:, columns], at_half, half_sem.at[c], 0, 1)

    rotate(final)
    for c in range(CHUNKS):
        columns = pl.ds(c * size, size)
        acc[:, columns] = acc[:, columns] + product(final, columns)
        half_out[:, columns] = acc[given, columns].astype(bf16)
        half_copy(c).start()
    for c in range(CHUNKS):
        columns = pl.ds(c * size, size)
        half_copy(c).wait_recv()
        term = acc[kept, columns] + half_in[:, columns].astype(f32)
        piece_out[:, :, columns] = term.astype(bf16).reshape(pieces, own, size)
        for k in range(pieces - 1, 0, -1):
            remote(
                piece_out.at[place ^ k, :, columns],
                piece_in.at[k, :, columns],
                at_piece,
                piece_sem.at[c],
                0,
                2 * k,
            ).start()
    others = pl.ds(1, pieces - 1)
    for c in range(CHUNKS):
        columns = pl.ds(c * size, size)
        some = piece_in.at[others, :, columns]
        remote(some, some, at_piece, piece_sem.at[c], 0, 2).wait_recv()
        term = piece_out[place, :, columns].astype(f32)
        for k in range(1, pieces):
            term = term + piece_in[k, :, columns].astype(f32)
        out[:, columns] = term.astype(bf16)

    for which, some in [
        (at_gather, gathered.at[pl.ds(0, len(sends))]),
        (at_core, core_out),
        (at_first, first_in),
        (at_half, half_out),
        (at_piece, piece_in.at[others]),
    ]:
        remote(some, some, which, core_sem.at[0], 0, 1).wait_send()
    for g in every:
        some = (second_in if quads[g] else second_out).at[:, :, down_rows(g)]
        remote(some, some, at_second + g, core_sem.at[0], 0, 1).wait_send()


def fused(n, tokens, gate_weight, up_weight, down_weight):
    own, depth = tokens.shape
    total = n * own
    part = gate_weight.shape[1] // 2
    blocks = part // COLS
    outs = down_weight.shape[1]
    ring = n // PLANE
    levels = ring.bit_length() - 1
    pieces = n // 2
    groups = pl.cdiv(blocks, GROUP)
    bf16, f32 = jnp.bfloat16, jnp.float32
    vmem = pl.BlockSpec(memory_space=pltpu.VMEM)
    anywhere = pl.BlockSpec(memory_space=pl.ANY)
    dma = pltpu.SemaphoreType.DMA
    return pl.pallas_call(
        functools.partial(kernel, n),
        out_shape=jax.ShapeDtypeStruct((own, outs), bf16),
        in_specs=[vmem, anywhere, anywhere, anywhere],
        out_specs=vmem,
        scratch_shapes=[
            pltpu.VMEM((2 * n, own, depth), bf16),
            pltpu.VMEM((2 * total, depth), bf16),
            pltpu.VMEM((total, outs), f32),
            pltpu.VMEM((blocks, depth, 2 * COLS), bf16),
            pltpu.VMEM((2 * part, outs), bf16),
            pltpu.VMEM((COLS, COLS), bf16),
            pltpu.VMEM((2, total, part), f32),
            pltpu.VMEM((2, total, part), bf16),
            pltpu.VMEM((2, total, part), bf16),
            pltpu.VMEM((2, total, part), bf16),
            pltpu.VMEM((3, total, part), bf16),
            pltpu.VMEM((total, 2 * part), f32),
            pltpu.VMEM((levels, total, 2 * part), bf16),
            pltpu.VMEM((ring - 1, total, 2 * part), bf16),
            pltpu.VMEM((total, 2 * part), bf16),
            pltpu.VMEM((total // 2, outs), bf16),
            pltpu.VMEM((total // 2, outs), bf16),
            pltpu.VMEM((pieces, own, outs), bf16),
            pltpu.VMEM((pieces, own, outs), bf16),
            dma((groups,)),
            dma((groups,)),
            dma((2 * ring + 2,)),
            dma((blocks,)),
            dma((groups,)),
            dma((groups, levels)),
            dma((CHUNKS,)),
            dma((CHUNKS,)),
            dma((5 + groups,)),
            pltpu.SemaphoreType.REGULAR,
        ],
        compiler_params=pltpu.CompilerParams(
            collective_id=0, has_side_effects=True, vmem_limit_bytes=67_000_000
        ),
    )(tokens, gate_weight, up_weight, down_weight)


def per_device(tokens, gate_weight, up_weight, down_weight):
    n, parts = lax.axis_size("tensor"), lax.axis_size("groups")
    own, depth = tokens.shape
    width, outs = gate_weight.shape[1], down_weight.shape[1]
    total = n * own
    held = 2 * (width * (depth + outs) + 4 * total * (depth + outs) + 20 * total * width)
    fits = (
        parts == 2
        and n in (8, 16)
        and width % (2 * COLS) == 0
        and width // (2 * COLS) > GROUP
        and total % 32 == 0
        and total <= 64
        and depth % (1024 * SPLIT) == 0
        and outs % (2048 * CHUNKS) == 0
        and held <= 68_000_000
    )
    if fits:
        return fused(n, tokens, gate_weight, up_weight, down_weight)
    return plain(tokens, gate_weight, up_weight, down_weight)


def solution(mesh):
    return jax.shard_map(
        per_device,
        mesh=mesh,
        in_specs=(
            P(("groups", "tensor"), None),
            P(None, "tensor"),
            P(None, "tensor"),
            P("tensor", None),
        ),
        out_specs=P(("groups", "tensor"), None),
        check_vma=False,
    )
```

time: 49.8 us -> 46.2 us (0.928)
  Pallas kernels: 48.1 us -> 44.6 us
    pallas_call x1, Pallas kernels: 48.1 us -> 44.6 us  [fused(): pl.pallas_call(functools.partial(kernel, n), out_shape=jax.ShapeDtypeStru...]
where the time goes in v2:
time: 46.2 us; the launch traced here: 46 us
  Pallas kernels  44.6 us (97%)
  local copies, waits for them, and re-layouts  1.4 us (3%)
    pallas_call x1, Pallas kernels, fused(): pl.pallas_call(functools.partial(kernel, n), out_shape=jax.ShapeDtypeStru...  44.6 us
    unnamed x1, local copies, waits for them, and re-layouts  1.4 us

profile of v2, /device:TPU:0, one launch (start us, length us, event | category | flops | bytes accessed | tf_op | source)
XLA Modules:
  0.0 46.0 jit_solution(188807873151654095)
XLA Ops:
  0.0 44.6 %shard_map.46 = bf16[2,8192]{1,0:T(2,128)(2,1)} custom-call(bf16[2,8192]{1,0:T(2,128)(2,1)} %tokens.1, bf16[8192,1792]{1,0:T(8,128)(2,1)} %gate.1, bf16[8192,1792]{1,0:T(8,128)(2,1)} %up.1, bf16[1792,8192]{1,0:T(8,128)(2,1)} %down.1), custom_call_target="tpu_custom_call" | custom-call | tf_op jit(solution)/shard_map/pallas_call | solution.py:497
  44.6 1.4 %copy.6 = bf16[2,8192]{1,0:T(2,128)(2,1)} copy(bf16[2,8192]{1,0:T(2,128)(2,1)} %shard_map.46) | data formatting | bytes 65536

commit v3 on v2

--- a/solution.py
+++ b/solution.py
@@ -14,7 +14,8 @@
 CHUNKS = 4
 GROUP = 2
 LAG = 1
-QUADS = (0, 3)
+QUADS = (0, 2, 3)
+WIDE = 128
 PLANE = 4
 MESH = pl.DeviceIdType.MESH
 
@@ -90,6 +91,7 @@
     second_out,
     second_in,
     rotated,
+    result,
     half_out,
     half_in,
     piece_out,
@@ -103,6 +105,7 @@
     half_sem,
     piece_sem,
     send_sem,
+    own_sem,
     known,
 ):
     f32, bf16 = jnp.float32, jnp.bfloat16
@@ -147,6 +150,9 @@
     greeted = plane + line[:2]
     for j, mask in greeted:
         pl.semaphore_signal(barrier, inc=1, device_id=device(j, mask), device_id_type=MESH)
+    loaded = pltpu.make_async_copy(tokens, gathered.at[slot(0, 0)], own_sem.at[0])
+    loaded.start()
+    loaded.wait()
 
     for g, (lo, hi) in enumerate(groups):
         for b in range(lo, hi):
@@ -199,8 +205,7 @@
     def send(origin, j, mask):
         place = slot(*origin)
         kind = kinds[origin[0] ^ j, origin[1] ^ mask]
-        source = gathered.at[place] if any(origin) else tokens
-        remote(source, gathered.at[place], at_gather, gather_sem.at[kind], j, mask).start()
+        remote(gathered.at[place], gathered.at[place], at_gather, gather_sem.at[kind], j, mask).start()
         sends.append(origin)
 
     def arrived(kind, count):
@@ -209,7 +214,6 @@
 
     for j, mask in [diagonal] + line[:2][::-1] + across + [(0, 1)]:
         send((0, 0), j, mask)
-    gathered[slot(0, 0)] = tokens[...]
     for j, mask in line[2:]:
         pl.semaphore_wait(known, 1)
         send((0, 0), j, mask)
@@ -387,11 +391,8 @@
         if level < levels - 1:
             second_copy(g, level + 1).start()
 
-    ready = project(0)
     for b in range(blocks):
-        later = project(b + 1) if b + 1 < blocks else None
-        block(b, *ready)
-        ready = later
+        block(b, *project(b))
         if b >= LAG:
             join(b - LAG)
     for b in range(max(blocks - LAG, 0), blocks):
@@ -417,12 +418,12 @@
         return jnp.dot(rotated[:, down_rows(g)], downs[down_rows(g), columns], preferred_element_type=f32)
 
     final = len(groups) - 1
-    for g in range(final):
+    for place, g in enumerate(sorted(range(final), key=lambda g: (not quads[g], g))):
         rotate(g)
-        for c in range(outs // 1024):
-            columns = pl.ds(c * 1024, 1024)
+        for c in range(outs // WIDE):
+            columns = pl.ds(c * WIDE, WIDE)
             term = product(g, columns)
-            if g:
+            if place:
                 term = acc[:, columns] + term
             acc[:, columns] = term
 
@@ -440,7 +441,9 @@
     rotate(final)
     for c in range(CHUNKS):
         columns = pl.ds(c * size, size)
-        acc[:, columns] = acc[:, columns] + product(final, columns)
+        for d in range(size // WIDE):
+            narrow = pl.ds(c * size + d * WIDE, WIDE)
+            acc[:, narrow] = acc[:, narrow] + product(final, narrow)
         half_out[:, columns] = acc[given, columns].astype(bf16)
         half_copy(c).start()
     for c in range(CHUNKS):
@@ -465,7 +468,9 @@
         term = piece_out[place, :, columns].astype(f32)
         for k in range(1, pieces):
             term = term + piece_in[k, :, columns].astype(f32)
-        out[:, columns] = term.astype(bf16)
+        result[:, columns] = term.astype(bf16)
+        pltpu.make_async_copy(result.at[:, columns], out.at[:, columns], own_sem.at[1]).start()
+    pltpu.make_async_copy(result, out, own_sem.at[1]).wait()
 
     for which, some in [
         (at_gather, gathered.at[pl.ds(0, len(sends))]),
@@ -491,14 +496,13 @@
     pieces = n // 2
     groups = pl.cdiv(blocks, GROUP)
     bf16, f32 = jnp.bfloat16, jnp.float32
-    vmem = pl.BlockSpec(memory_space=pltpu.VMEM)
     anywhere = pl.BlockSpec(memory_space=pl.ANY)
     dma = pltpu.SemaphoreType.DMA
     return pl.pallas_call(
         functools.partial(kernel, n),
         out_shape=jax.ShapeDtypeStruct((own, outs), bf16),
-        in_specs=[vmem, anywhere, anywhere, anywhere],
-        out_specs=vmem,
+        in_specs=[anywhere] * 4,
+        out_specs=anywhere,
         scratch_shapes=[
             pltpu.VMEM((2 * n, own, depth), bf16),
             pltpu.VMEM((2 * total, depth), bf16),
@@ -515,6 +519,7 @@
             pltpu.VMEM((levels, total, 2 * part), bf16),
             pltpu.VMEM((ring - 1, total, 2 * part), bf16),
             pltpu.VMEM((total, 2 * part), bf16),
+            pltpu.VMEM((own, outs), bf16),
             pltpu.VMEM((total // 2, outs), bf16),
             pltpu.VMEM((total // 2, outs), bf16),
             pltpu.VMEM((pieces, own, outs), bf16),
@@ -528,6 +533,7 @@
             dma((CHUNKS,)),
             dma((CHUNKS,)),
             dma((5 + groups,)),
+            dma((2,)),
             pltpu.SemaphoreType.REGULAR,
         ],
         compiler_params=pltpu.CompilerParams(

time: 46.2 us -> 45.4 us (0.983)
  Pallas kernels: 44.6 us -> 43.7 us
    pallas_call x1, Pallas kernels: 44.6 us -> 43.7 us  [fused(): pl.pallas_call(functools.partial(kernel, n), out_shape=jax.ShapeDtypeStru...]
where the time goes in v3:
time: 45.4 us; the launch traced here: 45.1 us
  Pallas kernels  43.7 us (96%)
  local copies, waits for them, and re-layouts  1.4 us (3%)
    pallas_call x1, Pallas kernels, fused(): pl.pallas_call(functools.partial(kernel, n), out_shape=jax.ShapeDtypeStru...  43.7 us
    unnamed x1, local copies, waits for them, and re-layouts  1.4 us

profile of v3, /device:TPU:0, one launch (start us, length us, event | category | flops | bytes accessed | tf_op | source)
XLA Modules:
  0.0 45.1 jit_solution(12989619583706663700)
XLA Ops:
  0.0 43.7 %shard_map.46 = bf16[2,8192]{1,0:T(2,128)(2,1)} custom-call(bf16[2,8192]{1,0:T(2,128)(2,1)} %tokens.1, bf16[8192,1792]{1,0:T(8,128)(2,1)} %gate.1, bf16[8192,1792]{1,0:T(8,128)(2,1)} %up.1, bf16[1792,8192]{1,0:T(8,128)(2,1)} %down.1), custom_call_target="tpu_custom_call" | custom-call | tf_op jit(solution)/shard_map/pallas_call | solution.py:501
  43.7 1.4 %copy.6 = bf16[2,8192]{1,0:T(2,128)(2,1)} copy(bf16[2,8192]{1,0:T(2,128)(2,1)} %shard_map.46) | data formatting | bytes 65536

commit v4 on v3

--- a/solution.py
+++ b/solution.py
@@ -13,7 +13,7 @@
 SPLIT = 4
 CHUNKS = 4
 GROUP = 2
-LAG = 1
+LAG = 2
 QUADS = (0, 2, 3)
 WIDE = 128
 PLANE = 4

time: 45.4 us -> 44.6 us (0.982)
  Pallas kernels: 43.7 us -> 43 us
    pallas_call x1, Pallas kernels: 43.7 us -> 43 us  [fused(): pl.pallas_call(functools.partial(kernel, n), out_shape=jax.ShapeDtypeStru...]
where the time goes in v4:
time: 44.6 us; the launch traced here: 44.4 us
  Pallas kernels  43 us (96%)
  local copies, waits for them, and re-layouts  1.4 us (3%)
    pallas_call x1, Pallas kernels, fused(): pl.pallas_call(functools.partial(kernel, n), out_shape=jax.ShapeDtypeStru...  43 us
    unnamed x1, local copies, waits for them, and re-layouts  1.4 us

profile of v4, /device:TPU:0, one launch (start us, length us, event | category | flops | bytes accessed | tf_op | source)
XLA Modules:
  0.0 44.4 jit_solution(12692745867755911710)
XLA Ops:
  0.0 43.0 %shard_map.46 = bf16[2,8192]{1,0:T(2,128)(2,1)} custom-call(bf16[2,8192]{1,0:T(2,128)(2,1)} %tokens.1, bf16[8192,1792]{1,0:T(8,128)(2,1)} %gate.1, bf16[8192,1792]{1,0:T(8,128)(2,1)} %up.1, bf16[1792,8192]{1,0:T(8,128)(2,1)} %down.1), custom_call_target="tpu_custom_call" | custom-call | tf_op jit(solution)/shard_map/pallas_call | solution.py:501
  43.0 1.4 %copy.6 = bf16[2,8192]{1,0:T(2,128)(2,1)} copy(bf16[2,8192]{1,0:T(2,128)(2,1)} %shard_map.46) | data formatting | bytes 65536
